TPU v7x, 32 devices: a whole 2x2x4 slice. The times are simulated.
32 devices in a mesh: dp: 4 (over y, x), expert: 8 (over z, core).
Axes of the slice: x: 2, y: 2, z: 4, core: 2. Of those that a mesh axis runs over, the one named last changes fastest.
Arguments:
- tokens: bfloat16 [4096, 2048], P(('dp', 'expert')), may hold values from -70 to 70
- routing: int32 [4096, 2], P(('dp', 'expert')), may hold values from 0 to 7, all different within a row; in each aligned block of 128 rows (0 to 127, 128 to 255, ...) at most 40 rows name the same one
- probs: bfloat16 [4096, 2], P(('dp', 'expert')), may hold values from 0.099609375 to 1
- cotangent: bfloat16 [4096, 2048], P(('dp', 'expert')), may hold values from -70 to 70
- w_gate: bfloat16 [8, 2048, 512], P('expert'), may hold values from -0.125 to 0.125
- w_up: bfloat16 [8, 2048, 512], P('expert'), may hold values from -0.125 to 0.125
- w_down: bfloat16 [8, 512, 2048], P('expert'), may hold values from -0.25 to 0.25
Outputs:
- grad_gate: float32 [8, 2048, 512], P('expert', 'dp')
- grad_up: float32 [8, 2048, 512], P('expert', 'dp')
- grad_down: float32 [8, 512, 2048], P('expert', None, 'dp')
- input_grad: bfloat16 [4096, 2048], P(('dp', 'expert'))
- router_grad: bfloat16 [4096, 2], P(('dp', 'expert'))
Inputs may be any that keep to these rules, and one draw needn't show every extreme that they name: `routing`: each row names 2 different experts. Among the 128 rows of one device no expert is named more than 40 times, a bound that some block reaches.
All inputs are finite; a program needn't handle non-finite values.
Results may differ from a plain program's by a relative error of at most 0.0065.
Values may be sent and summed in bfloat16 or wider, within the bound.
A program may use at most 64 MiB of HBM per device.

v0:
```python
import jax
import jax.numpy as jnp
from jax import lax
from jax.sharding import PartitionSpec as P

epsilon = 1e-06


def partner_2(value, axis, stride):
    mask = 2**stride
    pairs = [(source, source ^ mask) for source in range(lax.axis_size(axis))]
    return lax.ppermute(value, axis, pairs)


def contract(former, latter, former_dim, latter_dim):
    return lax.dot_general(
        former,
        latter,
        (((former_dim,), (latter_dim,)), ((), ())),
        preferred_element_type=jnp.float32,
    )


def expert_pass(routed, cot_rows, prob_rows, gate_matrix, up_matrix, down_matrix):
    gate_pre = jnp.dot(routed, gate_matrix, preferred_element_type=jnp.float32)
    up_pre = jnp.dot(routed, up_matrix, preferred_element_type=jnp.float32)
    sigmoid = jax.nn.sigmoid(gate_pre)
    activated = gate_pre * sigmoid
    hidden = (activated * up_pre).astype(jnp.bfloat16)
    output = jnp.dot(hidden, down_matrix, preferred_element_type=jnp.float32)
    router_slots = jnp.sum(output * cot_rows.astype(jnp.float32), axis=1).astype(jnp.bfloat16)
    scaled = (prob_rows.astype(jnp.float32)[:, None] * cot_rows.astype(jnp.float32)).astype(
        jnp.bfloat16
    )
    hidden_grad = contract(scaled, down_matrix, 1, 1)
    up_grad = (hidden_grad * activated).astype(jnp.bfloat16)
    gate_grad = (hidden_grad * up_pre * sigmoid * (1.0 + gate_pre * (1.0 - sigmoid))).astype(
        jnp.bfloat16
    )
    routed_grad = (
        contract(gate_grad, gate_matrix, 1, 1) + contract(up_grad, up_matrix, 1, 1)
    ).astype(jnp.bfloat16)
    return (hidden, scaled, gate_grad, up_grad, routed_grad, router_slots)


def weight_grads(routed, scaled, gate_grad, up_grad, hidden, scaling):
    return (
        jnp.stack(
            [
                contract(routed, gate_grad, 0, 0),
                contract(routed, up_grad, 0, 0),
                contract(scaled, hidden, 0, 0),
            ]
        )
        * scaling
    )


def split_halves(portion, own_bit):
    halfway = portion.shape[1] // 2
    retained = lax.dynamic_slice_in_dim(portion, own_bit * halfway, halfway, 1)
    handed = lax.dynamic_slice_in_dim(portion, (1 - own_bit) * halfway, halfway, 1)
    return (retained, handed)


def group_totals(totals, which_bit):
    position = lax.axis_index("dp")
    gathered = lax.all_gather(totals[None], "dp", axis=0, tiled=True)
    lowmask = (1 << which_bit) - 1
    indices = jnp.arange(gathered.shape[0], dtype=jnp.int32)
    member = (jnp.bitwise_and(indices, lowmask) == jnp.bitwise_and(position, lowmask)).astype(
        jnp.float32
    )
    return jnp.sum(gathered * member[:, None, None], axis=0)


def adasum_pair(retained, partner, own_bit, which_bit):
    own_sq = jnp.sum(retained * retained, axis=(1, 2))
    partner_sq = jnp.sum(partner * partner, axis=(1, 2))
    inner_sum = jnp.sum(retained * partner, axis=(1, 2))
    is_former = own_bit == 0
    former_sq = jnp.where(is_former, own_sq, partner_sq)
    latter_sq = jnp.where(is_former, partner_sq, own_sq)
    totals = jnp.stack([former_sq, latter_sq, inner_sum])
    totals = group_totals(totals, which_bit)
    former_coef = 1.0 - totals[2] / (2.0 * (totals[0] + epsilon))
    latter_coef = 1.0 - totals[2] / (2.0 * (totals[1] + epsilon))
    own_coef = jnp.where(is_former, former_coef, latter_coef)
    partner_coef = jnp.where(is_former, latter_coef, former_coef)
    return own_coef[:, None, None] * retained + partner_coef[:, None, None] * partner


def per_device(tokens, routing, probs, cotangent, w_gate, w_up, w_down):
    experts = lax.axis_size("expert")
    rows_here, top_count = routing.shape
    model_width = tokens.shape[1]
    capacity = 5 * rows_here * top_count // (4 * experts)
    choices = rows_here * top_count
    slot_total = experts * capacity
    flattened = routing.reshape(-1)
    onehot = (flattened[:, None] == jnp.arange(experts, dtype=jnp.int32)[None, :]).astype(jnp.int32)
    before = jnp.cumsum(onehot, axis=0) - onehot
    destination = flattened * capacity + jnp.sum(before * onehot, axis=1)
    source = (
        jnp.full((slot_total,), choices, jnp.int32)
        .at[destination]
        .set(jnp.arange(choices, dtype=jnp.int32))
    )
    token_of = jnp.where(source < choices, source // top_count, rows_here)
    send_rows = jnp.take(tokens, token_of, axis=0, mode="fill", fill_value=0)
    send_cot = jnp.take(cotangent, token_of, axis=0, mode="fill", fill_value=0)
    send_prob = jnp.take(probs.reshape(-1), source, axis=0, mode="fill", fill_value=0)
    routed, cot_rows, prob_rows = (
        lax.all_to_all(
            send_rows.reshape(experts, capacity, model_width),
            "expert",
            split_axis=0,
            concat_axis=0,
            tiled=True,
        ),
        lax.all_to_all(
            send_cot.reshape(experts, capacity, model_width),
            "expert",
            split_axis=0,
            concat_axis=0,
            tiled=True,
        ),
        lax.all_to_all(
            send_prob.reshape(experts, capacity), "expert", split_axis=0, concat_axis=0, tiled=True
        ),
    )
    routed = routed.reshape(slot_total, model_width)
    cot_rows = cot_rows.reshape(slot_total, model_width)
    prob_rows = prob_rows.reshape(slot_total)
    hidden, scaled, gate_grad, up_grad, routed_grad, router_slots = expert_pass(
        routed, cot_rows, prob_rows, w_gate[0], w_up[0], w_down[0]
    )
    arrived_grad, arrived_router = (
        lax.all_to_all(
            routed_grad.reshape(experts, capacity, model_width),
            "expert",
            split_axis=0,
            concat_axis=0,
            tiled=True,
        ),
        lax.all_to_all(
            router_slots.reshape(experts, capacity),
            "expert",
            split_axis=0,
            concat_axis=0,
            tiled=True,
        ),
    )
    picked = arrived_grad.reshape(slot_total, model_width)[destination]
    input_grad = jnp.sum(
        picked.reshape(rows_here, top_count, model_width).astype(jnp.float32), axis=1
    )
    input_grad = input_grad.astype(jnp.bfloat16)
    router_grad = arrived_router.reshape(slot_total)[destination].reshape(rows_here, top_count)
    scaling = 1.0 / slot_total
    levels = lax.axis_size("dp").bit_length() - 1
    position = lax.axis_index("dp")
    top_bit = position >> levels - 1 & 1
    halfway = model_width // 2
    hidden_width = hidden.shape[1]
    routed_kept = lax.dynamic_slice_in_dim(routed, top_bit * halfway, halfway, 1)
    routed_handed = lax.dynamic_slice_in_dim(routed, (1 - top_bit) * halfway, halfway, 1)
    scaled_kept = lax.dynamic_slice_in_dim(scaled, top_bit * halfway, halfway, 1)
    scaled_handed = lax.dynamic_slice_in_dim(scaled, (1 - top_bit) * halfway, halfway, 1)
    retained = weight_grads(routed_kept, scaled_kept, gate_grad, up_grad, hidden, scaling)
    bundle = jnp.concatenate([routed_handed, scaled_handed, gate_grad, up_grad, hidden], axis=1)
    received = partner_2(bundle, "dp", levels - 1)
    mark = 2 * halfway
    partner = weight_grads(
        received[:, :halfway],
        received[:, halfway:mark],
        received[:, mark : mark + hidden_width],
        received[:, mark + hidden_width : mark + 2 * hidden_width],
        received[:, mark + 2 * hidden_width :],
        scaling,
    )
    portion = adasum_pair(retained, partner, top_bit, levels - 1)
    for halving in range(1, levels):
        which_bit = levels - 1 - halving
        own_bit = position >> which_bit & 1
        retained, handed = split_halves(portion, own_bit)
        partner = partner_2(handed.astype(jnp.bfloat16), "dp", which_bit).astype(handed.dtype)
        portion = adasum_pair(retained, partner, own_bit, which_bit)
    return (portion[0][None], portion[1][None], portion[2].T[None], input_grad, router_grad)


def solution(mesh):
    placed = (
        P(("dp", "expert"), None),
        P(("dp", "expert"), None),
        P(("dp", "expert"), None),
        P(("dp", "expert"), None),
        P("expert", None, None),
        P("expert", None, None),
        P("expert", None, None),
    )
    return jax.shard_map(
        per_device,
        mesh=mesh,
        in_specs=placed,
        out_specs=(
            P("expert", "dp", None),
            P("expert", "dp", None),
            P("expert", None, "dp"),
            P(("dp", "expert"), None),
            P(("dp", "expert"), None),
        ),
        check_vma=False,
    )
```

profile of v0, /device:TPU:12, one launch (start us, length us, event | category | flops | bytes accessed | tf_op | source)
XLA Modules:
  0.0 247.8 jit_solution(16819925488629433948)
XLA Ops:
  9.3 5.3 %all-to-all-start.1 = ((bf16[8,1,40]{2,1,0:T(2,128)(2,1)}), bf16[8,1,40]{2,1,0:T(2,128)(2,1)S(1)}, u32[]{:S(2)}, u32[]{:S(2)}) async-start(bf16[8,1,40]{2,1,0:T(2,128)(2,1)} %select_n.188), calls=%async_computation.1 | async-start | bytes 8192 | tf_op jit(solution)/shard_map/all_to_all | solution.py:128
  14.6 3.0 %gather_fusion.4 = bf16[320,2048]{1,0:T(8,128)(2,1)} fusion(bf16[128,2048]{1,0:T(8,128)(2,1)S(1)} %copy-done.1, s32[1024]{0:T(1024)S(1)} %get-tuple-element.59), kind=kCustom, calls=%fused_computation.1.clone | custom fusion | bytes 2622720 | tf_op jit(solution)/shard_map/jit(_take)/gather | solution.py:111
  17.6 3.0 %gather_fusion.3 = bf16[320,2048]{1,0:T(8,128)(2,1)} fusion(bf16[128,2048]{1,0:T(8,128)(2,1)S(1)} %copy-done.2, s32[1024]{0:T(1024)S(1)} %get-tuple-element.59), kind=kCustom, calls=%fused_computation.clone | custom fusion | bytes 2622720 | tf_op jit(solution)/shard_map/jit(_take)/gather | solution.py:110
  20.6 3.0 %broadcast_select_fusion = (bf16[320,2048]{1,0:T(8,128)(2,1)}, bf16[320,2048]{1,0:T(8,128)(2,1)S(1)}) fusion(bf16[320,2048]{1,0:T(8,128)(2,1)} %gather_fusion.4, pred[320]{0:T(512)(128)(4,1)S(1)} %get-tuple-element.46, bf16[320,2048]{1,0:T(8,128)(2,1)} %gather_fusion.3), kind=kLoop, calls=%fused_computation.42 | loop fusion | flops 1310720 | bytes 5243200 | tf_op jit(solution)/shard_map/jit(_take)/select_n | solution.py:111
  23.7 34.9 %all_to_all.27 = bf16[8,40,2048]{2,1,0:T(8,128)(2,1)} all-to-all(bf16[8,40,2048]{2,1,0:T(8,128)(2,1)S(1)} %bitcast.97), channel_id=1, replica_groups=mesh['dp'=4,'expert'=8] {'expert'}, dimensions={0} | all-to-all | bytes 2621440 | tf_op jit(solution)/shard_map/all_to_all | solution.py:114
  58.5 5.8 %all-to-all-start.2 = ((bf16[8,40,2048]{2,1,0:T(8,128)(2,1)}), bf16[8,40,2048]{2,1,0:T(8,128)(2,1)S(1)}, u32[]{:S(2)}, u32[]{:S(2)}) async-start(bf16[8,40,2048]{2,1,0:T(8,128)(2,1)} %bitcast.96), calls=%async_computation.2 | async-start | bytes 2621440 | tf_op jit(solution)/shard_map/all_to_all | solution.py:121
  66.4 3.7 %fusion.9 = f32[320,512]{1,0:T(8,128)} fusion(bf16[320,2048]{1,0:T(8,128)(2,1)} %bitcast.91, bf16[1,2048,512]{2,1,0:T(8,128)(2,1)} %param.14), kind=kOutput, calls=%fused_computation.30 | convolution fusion | flops 671088640 | bytes 4063232 | tf_op jit(solution)/shard_map/dot_general | solution.py:26
  70.1 22.9 %all-to-all-done.2 = bf16[8,40,2048]{2,1,0:T(8,128)(2,1)S(1)} async-done(((bf16[8,40,2048]{2,1,0:T(8,128)(2,1)}), bf16[8,40,2048]{2,1,0:T(8,128)(2,1)S(1)}, u32[]{:S(2)}, u32[]{:S(2)}) %all-to-all-start.2) | async-done | bytes 1310752 | tf_op jit(solution)/shard_map/all_to_all | solution.py:121
  103.0 3.3 %fusion.14 = bf16[320]{0:T(512)(128)(2,1)S(1)} fusion(f32[320,2048]{1,0:T(8,128)} %bitcast.89, bf16[320,512]{1,0:T(8,128)(2,1)S(1)} %get-tuple-element.39, bf16[1,512,2048]{2,1,0:T(8,128)(2,1)} %param.15), kind=kOutput, calls=%fused_computation.41 | convolution fusion | flops 672399040 | bytes 5046912 | tf_op jit(solution)/shard_map/dot_general | solution.py:30
  107.0 6.7 %all-to-all-start.4 = ((bf16[8,1,40]{2,1,0:T(2,128)(2,1)}), bf16[8,1,40]{2,1,0:T(2,128)(2,1)S(1)}, u32[]{:S(2)}, u32[]{:S(2)}) async-start(bf16[8,1,40]{2,1,0:T(2,128)(2,1)} %convert_element_type.106), calls=%async_computation.4 | async-start | bytes 8192 | tf_op jit(solution)/shard_map/all_to_all | solution.py:146
  118.5 35.8 %collective-permute-done = bf16[320,3584]{1,0:T(8,128)(2,1)} collective-permute-done((bf16[320,3584]{1,0:T(8,128)(2,1)}, bf16[320,3584]{1,0:T(8,128)(2,1)}, u32[]{:S(2)}, u32[]{:S(2)}) %collective-permute-start) | collective-permute-done | bytes 2293792 | tf_op jit(solution)/shard_map/ppermute | solution.py:12
  156.3 2.6 %convolution_bitcast_fusion = f32[1,1024,512]{2,1,0:T(8,128)S(1)} fusion(bf16[320,3584]{1,0:T(8,128)(2,1)} %collective-permute-done), kind=kOutput, calls=%fused_computation.35 | convolution fusion | flops 335544320 | bytes 3080192 | tf_op jit(solution)/shard_map/dot_general | solution.py:16
  159.0 2.6 %convolution_bitcast_fusion.2 = f32[1,1024,512]{2,1,0:T(8,128)S(1)} fusion(bf16[320,3584]{1,0:T(8,128)(2,1)} %collective-permute-done), kind=kOutput, calls=%fused_computation.37 | convolution fusion | flops 335544320 | bytes 3080192 | tf_op jit(solution)/shard_map/dot_general | solution.py:16
  161.7 2.9 %multiply_reduce_fusion.2 = (f32[3]{0:T(128)S(1)}, f32[3]{0:T(128)S(1)}, f32[3]{0:T(128)S(1)}) fusion(f32[1,1024,512]{2,1,0:T(8,128)S(1)} %convolution_bitcast_fusion.3, f32[1,1024,512]{2,1,0:T(8,128)S(1)} %convolution_bitcast_fusion.4, f32[1,1024,512]{2,1,0:T(8,128)S(1)} %convolution_bitcast_fusion.5, f32[1,1024,512]{2,1,0:T(8,128)S(1)} %convolution_bitcast_fusion, ...), kind=kLoop, calls=%fused_computation.11 | loop fusion | flops 18874360 | bytes 12582948 | tf_op jit(solution)/shard_map/reduce_sum | solution.py:78
  166.6 8.1 %all-gather.2 = f32[4,3,3]{2,1,0:T(4,128)S(1)} all-gather(f32[1,3,3]{2,1,0:T(4,128)S(1)} %maximum_bitcast_fusion), channel_id=2, replica_groups=mesh['dp'=4,'expert'=8] {'dp'}, dimensions={0}, use_global_device_ids=true | all-gather | bytes 180 | tf_op jit(solution)/shard_map/all_gather | solution.py:68
  174.7 6.4 %all-to-all-start.3 = ((bf16[8,40,2048]{2,1,0:T(8,128)(2,1)}), bf16[8,40,2048]{2,1,0:T(8,128)(2,1)S(1)}, u32[]{:S(2)}, u32[]{:S(2)}) async-start(bf16[8,40,2048]{2,1,0:T(8,128)(2,1)} %bitcast.95), calls=%async_computation.3 | async-start | bytes 2621440 | tf_op jit(solution)/shard_map/all_to_all | solution.py:139
  181.2 5.7 %multiply_add_fusion = f32[3,1024,512]{2,1,0:T(8,128)S(1)} fusion(f32[3]{0:T(128)S(1)} %fusion.47, f32[3]{0:T(128)S(1)} %get-tuple-element.35, f32[1,1024,512]{2,1,0:T(8,128)} %copy-done.8, f32[1,1024,512]{2,1,0:T(8,128)} %copy-done.7, f32[1,1024,512]{2,1,0:T(8,128)} %copy-done.9, f32[1,1024,512]{2,1,0:T(8,128)} %copy-done.4, f32[1,1024,512]{2,1,0:T(8,128)} %copy-done.5, ...), kind=kLoop, calls=%fused_computation.8 | loop fusion | flops 11010048 | bytes 18874392 | tf_op jit(solution)/shard_map/add | solution.py:90
  186.9 2.7 %copy-done.3 = f32[3,1024,512]{2,1,0:T(8,128)} copy-done((f32[3,1024,512]{2,1,0:T(8,128)}, f32[3,1024,512]{2,1,0:T(8,128)S(1)}, u32[]{:S(2)}) %copy-start.3) | copy-done | bytes 6291480
  194.3 15.6 %all-to-all-done.3 = bf16[8,40,2048]{2,1,0:T(8,128)(2,1)S(1)} async-done(((bf16[8,40,2048]{2,1,0:T(8,128)(2,1)}), bf16[8,40,2048]{2,1,0:T(8,128)(2,1)S(1)}, u32[]{:S(2)}, u32[]{:S(2)}) %all-to-all-start.3) | async-done | bytes 1310752 | tf_op jit(solution)/shard_map/all_to_all | solution.py:139
  214.0 13.7 %collective-permute-done.1 = bf16[3,512,512]{2,1,0:T(8,128)(2,1)} collective-permute-done((bf16[3,512,512]{2,1,0:T(8,128)(2,1)}, bf16[3,512,512]{2,1,0:T(8,128)(2,1)}, u32[]{:S(2)}, u32[]{:S(2)}) %collective-permute-start.1) | collective-permute-done | bytes 1572896 | tf_op jit(solution)/shard_map/ppermute | solution.py:12
  227.7 3.4 %multiply_reduce_fusion.3 = (f32[3]{0:T(128)S(1)}, f32[3]{0:T(128)S(1)}, f32[3]{0:T(128)S(1)}) fusion(f32[3,1024,512]{2,1,0:T(8,128)} %copy-done.3, s32[]{:T(128)S(6)} %select_n.170, bf16[3,512,512]{2,1,0:T(8,128)(2,1)} %collective-permute-done.1), kind=kLoop, calls=%fused_computation.19 | loop fusion | flops 5505015 | bytes 4718632 | tf_op jit(solution)/shard_map/reduce_sum | solution.py:78
  231.1 3.6 %reduce_sum.114 = bf16[128,2048]{1,0:T(8,128)(2,1)} reduce(bf16[128,2,2048]{2,1,0:T(2,128)(2,1)S(1)} %reshape.319, bf16[]{:T(256)} %constant.71.clone.1), dimensions={1}, to_apply=%region_12.14 | reduce | flops 262144 | bytes 1572866 | tf_op jit(solution)/shard_map/reduce_sum | solution.py:155
  234.8 7.1 %all-gather.3 = f32[4,3,3]{2,1,0:T(4,128)S(1)} all-gather(f32[1,3,3]{2,1,0:T(4,128)S(1)} %maximum_bitcast_fusion.1), channel_id=3, replica_groups=mesh['dp'=4,'expert'=8] {'dp'}, dimensions={0}, use_global_device_ids=true | all-gather | bytes 180 | tf_op jit(solution)/shard_map/all_gather | solution.py:68
  241.9 3.0 %fusion.2 = f32[3,512,512]{2,1,0:T(8,128)S(1)} fusion(bf16[3,512,512]{2,1,0:T(8,128)(2,1)} %collective-permute-done.1, f32[3,1024,512]{2,1,0:T(8,128)} %copy-done.3, s32[]{:T(128)S(6)} %select_n.170, f32[3]{0:T(128)S(1)} %fusion.43, f32[3]{0:T(128)S(1)} %get-tuple-element.32), kind=kLoop, calls=%fused_computation.17 | loop fusion | flops 3145728 | bytes 7864348 | tf_op jit(solution)/shard_map/add | solution.py:90
  (104 shorter events, 41.8 us)
Async XLA Ops:
  0.6 97.7 %copy-start = (bf16[1,2048,512]{2,1,0:T(8,128)(2,1)S(1)}, bf16[1,2048,512]{2,1,0:T(8,128)(2,1)}, u32[]{:S(2)}) copy-start(bf16[1,2048,512]{2,1,0:T(8,128)(2,1)} %param.13) | copy-start | bytes 6291460
  0.6 13.9 %copy-start.1 = (bf16[128,2048]{1,0:T(8,128)(2,1)S(1)}, bf16[128,2048]{1,0:T(8,128)(2,1)}, u32[]{:S(2)}) copy-start(bf16[128,2048]{1,0:T(8,128)(2,1)} %param.12) | copy-start | bytes 1572868
  9.3 14.4 %all-to-all-start.1 = ((bf16[8,1,40]{2,1,0:T(2,128)(2,1)}), bf16[8,1,40]{2,1,0:T(2,128)(2,1)S(1)}, u32[]{:S(2)}, u32[]{:S(2)}) async-start(bf16[8,1,40]{2,1,0:T(2,128)(2,1)} %select_n.188), calls=%async_computation.1 | async-start | bytes 8192 | tf_op jit(solution)/shard_map/all_to_all | solution.py:128
  14.6 3.0 %copy-start.2 = (bf16[128,2048]{1,0:T(8,128)(2,1)S(1)}, bf16[128,2048]{1,0:T(8,128)(2,1)}, u32[]{:S(2)}) copy-start(bf16[128,2048]{1,0:T(8,128)(2,1)} %param.9) | copy-start | bytes 1572868
  58.5 34.5 %all-to-all-start.2 = ((bf16[8,40,2048]{2,1,0:T(8,128)(2,1)}), bf16[8,40,2048]{2,1,0:T(8,128)(2,1)S(1)}, u32[]{:S(2)}, u32[]{:S(2)}) async-start(bf16[8,40,2048]{2,1,0:T(8,128)(2,1)} %bitcast.96), calls=%async_computation.2 | async-start | bytes 2621440 | tf_op jit(solution)/shard_map/all_to_all | solution.py:121
  93.1 1.6 copy-start.17
  95.5 2.8 %copy-start.10 = (bf16[8,40,2048]{2,1,0:T(8,128)(2,1)S(1)}, bf16[8,40,2048]{2,1,0:T(8,128)(2,1)}, u32[]{:S(2)}) copy-start(bf16[8,40,2048]{2,1,0:T(8,128)(2,1)} %all_to_all.27) | copy-start | bytes 3932164
  95.5 2.8 %copy-start.18 = (f32[320,512]{1,0:T(8,128)S(1)}, f32[320,512]{1,0:T(8,128)}, u32[]{:S(2)}) copy-start(f32[320,512]{1,0:T(8,128)} %fusion.9) | copy-start | bytes 1966084
  97.3 2.9 %copy-start.12 = (bf16[320,2048]{1,0:T(8,128)(2,1)}, bf16[320,2048]{1,0:T(8,128)(2,1)S(1)}, u32[]{:S(2)}) copy-start(bf16[320,2048]{1,0:T(8,128)(2,1)S(1)} %get-tuple-element.44) | copy-start | bytes 3932164
  102.2 52.1 %collective-permute-start = (bf16[320,3584]{1,0:T(8,128)(2,1)}, bf16[320,3584]{1,0:T(8,128)(2,1)}, u32[]{:S(2)}, u32[]{:S(2)}) collective-permute-start(bf16[320,3584]{1,0:T(8,128)(2,1)} %get-tuple-element.38), channel_id=1, source_target_pairs={{0,16},{8,24},{16,0},{24,8},{1,17},{9,25},{17,1},{25,9},{2,18},{10... | collective-permute-start | bytes 6881288 | tf_op jit(solution)/shard_map/ppermute | solution.py:12
  106.3 9.4 %copy-start.11 = (bf16[8,40,2048]{2,1,0:T(8,128)(2,1)S(1)}, bf16[8,40,2048]{2,1,0:T(8,128)(2,1)}, u32[]{:S(2)}) copy-start(bf16[8,40,2048]{2,1,0:T(8,128)(2,1)} %all_to_all.27) | copy-start | bytes 3932164
  107.0 67.8 %all-to-all-start.4 = ((bf16[8,1,40]{2,1,0:T(2,128)(2,1)}), bf16[8,1,40]{2,1,0:T(2,128)(2,1)S(1)}, u32[]{:S(2)}, u32[]{:S(2)}) async-start(bf16[8,1,40]{2,1,0:T(2,128)(2,1)} %convert_element_type.106), calls=%async_computation.4 | async-start | bytes 8192 | tf_op jit(solution)/shard_map/all_to_all | solution.py:146
  113.7 2.0 copy-start.14
  115.6 46.0 %copy-start.4 = (f32[1,1024,512]{2,1,0:T(8,128)}, f32[1,1024,512]{2,1,0:T(8,128)S(1)}, u32[]{:S(2)}) copy-start(f32[1,1024,512]{2,1,0:T(8,128)S(1)} %convolution_bitcast_fusion.3) | copy-start | bytes 6291460
  115.6 1.2 copy-start.15
  116.4 45.2 %copy-start.5 = (f32[1,1024,512]{2,1,0:T(8,128)}, f32[1,1024,512]{2,1,0:T(8,128)S(1)}, u32[]{:S(2)}) copy-start(f32[1,1024,512]{2,1,0:T(8,128)S(1)} %convolution_bitcast_fusion.4) | copy-start | bytes 6291460
  117.6 44.0 %copy-start.6 = (f32[1,1024,512]{2,1,0:T(8,128)}, f32[1,1024,512]{2,1,0:T(8,128)S(1)}, u32[]{:S(2)}) copy-start(f32[1,1024,512]{2,1,0:T(8,128)S(1)} %convolution_bitcast_fusion.5) | copy-start | bytes 6291460
  156.3 5.4 %copy-start.7 = (f32[1,1024,512]{2,1,0:T(8,128)}, f32[1,1024,512]{2,1,0:T(8,128)S(1)}, u32[]{:S(2)}) copy-start(f32[1,1024,512]{2,1,0:T(8,128)S(1)} %convolution_bitcast_fusion.1) | copy-start | bytes 6291460
  159.0 5.6 %copy-start.8 = (f32[1,1024,512]{2,1,0:T(8,128)}, f32[1,1024,512]{2,1,0:T(8,128)S(1)}, u32[]{:S(2)}) copy-start(f32[1,1024,512]{2,1,0:T(8,128)S(1)} %convolution_bitcast_fusion) | copy-start | bytes 6291460
  161.7 2.9 %copy-start.9 = (f32[1,1024,512]{2,1,0:T(8,128)}, f32[1,1024,512]{2,1,0:T(8,128)S(1)}, u32[]{:S(2)}) copy-start(f32[1,1024,512]{2,1,0:T(8,128)S(1)} %convolution_bitcast_fusion.2) | copy-start | bytes 6291460
  161.7 2.9 %copy-start.16 = (bf16[1,2048,512]{2,1,0:T(8,128)(2,1)S(1)}, bf16[1,2048,512]{2,1,0:T(8,128)(2,1)}, u32[]{:S(2)}) copy-start(bf16[1,2048,512]{2,1,0:T(8,128)(2,1)} %param.14) | copy-start | bytes 6291460
  174.7 35.2 %all-to-all-start.3 = ((bf16[8,40,2048]{2,1,0:T(8,128)(2,1)}), bf16[8,40,2048]{2,1,0:T(8,128)(2,1)S(1)}, u32[]{:S(2)}, u32[]{:S(2)}) async-start(bf16[8,40,2048]{2,1,0:T(8,128)(2,1)} %bitcast.95), calls=%async_computation.3 | async-start | bytes 2621440 | tf_op jit(solution)/shard_map/all_to_all | solution.py:139
  186.9 2.7 %copy-start.3 = (f32[3,1024,512]{2,1,0:T(8,128)}, f32[3,1024,512]{2,1,0:T(8,128)S(1)}, u32[]{:S(2)}) copy-start(f32[3,1024,512]{2,1,0:T(8,128)S(1)} %multiply_add_fusion) | copy-start | bytes 18874372
  190.9 36.7 %collective-permute-start.1 = (bf16[3,512,512]{2,1,0:T(8,128)(2,1)}, bf16[3,512,512]{2,1,0:T(8,128)(2,1)}, u32[]{:S(2)}, u32[]{:S(2)}) collective-permute-start(bf16[3,512,512]{2,1,0:T(8,128)(2,1)} %dynamic-slice_convert_fusion), channel_id=1, source_target_pairs={{0,8},{8,0},{16,24},{24,16},{1,9},{9,1},{17,25},{25,17},{2,10},{10... | collective-permute-start | bytes 4718600 | tf_op jit(solution)/shard_map/ppermute | solution.py:12
  (1 other events, 0.7 us)
where the time goes:
time: 251 us; the launch traced here: 248 us
  waiting for transfers between devices  88.1 us (35%)
  blocking collectives  50 us (20%)
  local copies, waits for them, and re-layouts  32.5 us (13%)
  other arithmetic  27.5 us (11%)
  starting transfers between devices  25.3 us (10%)
  matrix products  23.3 us (9%)
    ppermute x2, waiting for transfers between devices, partner_2(): return lax.ppermute(value, axis, pairs)  49.5 us
    all_to_all x1, blocking collectives, per_device(): lax.all_to_all(send_rows.reshape(experts, capacity, model_width), 'expert...  34.9 us
    all_to_all x1, waiting for transfers between devices, per_device(): lax.all_to_all(send_cot.reshape(experts, capacity, model_width), 'expert'...  22.9 us
    all_to_all x1, waiting for transfers between devices, per_device(): lax.all_to_all(routed_grad.reshape(experts, capacity, model_width), 'expe...  15.6 us
    all_gather x2, blocking collectives, group_totals(): gathered = lax.all_gather(totals[None], 'dp', axis=0, tiled=True)  15.2 us
    dot_general x9, matrix products, contract(): lax.dot_general(former, latter, (((former_dim,), (latter_dim,)), ((), ())...  14.4 us
    unnamed x44, local copies, waits for them, and re-layouts  11.1 us
    add x2, other arithmetic, adasum_pair(): own_coef[:, None, None] * retained + partner_coef[:, None, None] * partner  8.62 us
  transfers between devices with their start and end apart: 6, of which 4 were waited for; matrix products, arithmetic and copies ran while one was open for 20% of the time, Pallas kernels for 0%

commit v1 on v0

v1 whole, which is shorter than its diff:
```python
import functools

import jax
import jax.numpy as jnp
from jax import lax
from jax.experimental import pallas as pl
from jax.experimental.pallas import tpu as pltpu
from jax.sharding import PartitionSpec as P

epsilon = 1e-06
MESH = pl.DeviceIdType.MESH
f32, bf16, i32 = jnp.float32, jnp.bfloat16, jnp.int32
ROWS = 128
LANES = 128


def dot(a, b, ad=1, bd=0):
    return lax.dot_general(a, b, (((ad,), (bd,)), ((), ())), preferred_element_type=f32)


def kernel(
    experts, replicas, cap, capp,
    tok, cot, rout, rout_t, prob_t, wg_hbm, wu_hbm, wd_hbm,
    out_gate, out_up, out_down, out_in, out_router,
    wg, wu, wd, ranks, weights, select, send_tok, send_cot, routed, cotp, scaled,
    gate_pre, up_pre, acts, p_routed, p_scaled, p_acts, ret_send, ret_recv,
    own, part, handed, landed, tot_send, tot_recv,
    w_sem, st_sem, rt_sem, sc_sem, rc_sem, sr_sem, rr_sem,
    yts_sem, ytr_sem, yss_sem, ysr_sem, yas_sem, yar_sem, xs_sem, xr_sem, ts_sem, tr_sem,
):
    me = lax.axis_index("expert")
    dp = lax.axis_index("dp")
    tokens, width = tok.shape
    hidden = wg.shape[1]
    slots = experts * capp
    levels = replicas.bit_length() - 1
    half = width // 2
    bits = [lax.rem(dp // (1 << b), 2) for b in range(levels)]
    mates = [dp + (1 << b) * (1 - 2 * bits[b]) for b in range(levels)]
    top = levels - 1
    order = sorted(range(1, experts), key=lambda i: abs(2 * i - experts))

    def block(index):
        return pl.ds(pl.multiple_of(index * capp, capp), capp)

    loads = [
        pltpu.make_async_copy(src.at[0], dst, w_sem.at[j])
        for j, (src, dst) in enumerate(((wg_hbm, wg), (wu_hbm, wu), (wd_hbm, wd)))
    ]
    for load in loads:
        load.start()

    barrier = pltpu.get_barrier_semaphore()
    for i in range(1, experts):
        pl.semaphore_signal(
            barrier, inc=1, device_id={"expert": lax.rem(me + i, experts)}, device_id_type=MESH
        )
    for mate in mates:
        pl.semaphore_signal(barrier, inc=1, device_id={"dp": mate}, device_id_type=MESH)

    first, second = rout_t[0:1, :], rout_t[1:2, :]
    names = lax.broadcasted_iota(i32, ranks.shape, 0)
    is_first, is_second = names == first, names == second
    member = jnp.where(is_first | is_second, 1.0, 0.0).astype(f32)
    earlier = lax.broadcasted_iota(i32, (tokens, tokens), 0)
    later = lax.broadcasted_iota(i32, (tokens, tokens), 1)
    before = dot(member.astype(bf16), jnp.where(earlier < later, 1.0, 0.0).astype(bf16))
    ranks[...] = jnp.where(member > 0.0, before, -1.0).astype(i32)
    weights[...] = jnp.where(
        is_first, prob_t[0:1, :], jnp.where(is_second, prob_t[1:2, :], 0.0)
    )
    slot = lax.broadcasted_iota(i32, (capp, tokens), 0)

    def picks(expert):
        return slot == ranks[pl.ds(expert, 1), :]

    pl.semaphore_wait(barrier, experts - 1 + levels)

    tok_copies, cot_copies = [], []
    for i in order:
        k = lax.rem(me + i, experts)
        chosen = jnp.where(picks(k), 1.0, 0.0).astype(bf16)
        select[block(k), :] = chosen
        send_tok[block(k), :] = dot(chosen, tok[...]).astype(bf16)
        copy = pltpu.make_async_remote_copy(
            send_tok.at[block(k)], routed.at[block(me)], st_sem.at[i], rt_sem.at[i],
            device_id={"expert": k}, device_id_type=MESH,
        )
        copy.start()
        tok_copies.append(copy)

    def fill_cot(target, k):
        picked = picks(k)
        chosen = jnp.where(picked, 1.0, 0.0).astype(bf16)
        weight = jnp.sum(
            jnp.where(picked, weights[pl.ds(k, 1), :], 0.0), axis=1, keepdims=True
        )
        target[block(k), 0:width] = dot(chosen, cot[...]).astype(bf16)
        target[block(k), width:] = jnp.broadcast_to(weight, (capp, LANES)).astype(bf16)
        return chosen

    for i in order:
        k = lax.rem(me + i, experts)
        fill_cot(send_cot, k)
        copy = pltpu.make_async_remote_copy(
            send_cot.at[block(k)], cotp.at[block(me)], sc_sem.at[i], rc_sem.at[i],
            device_id={"expert": k}, device_id_type=MESH,
        )
        copy.start()
        cot_copies.append(copy)
    mine = fill_cot(cotp, me)
    select[block(me), :] = mine
    routed[block(me), :] = dot(mine, tok[...]).astype(bf16)

    kept_at = pl.multiple_of(bits[top] * half, LANES)
    handed_at = pl.multiple_of((1 - bits[top]) * half, LANES)
    y_copies = []

    def to_mate(source, target, send_sem, recv_sem):
        copy = pltpu.make_async_remote_copy(
            source, target, send_sem, recv_sem, device_id={"dp": mates[top]}, device_id_type=MESH
        )
        copy.start()
        y_copies.append(copy)
        return copy

    tok_to_mate, sca_to_mate, act_to_mate = [], [], {}
    for position, i in enumerate([0] + order):
        k = lax.rem(me + experts - i, experts)
        if i:
            tok_copies[position - 1].wait_recv()
        tok_to_mate.append(to_mate(
            routed.at[block(k), pl.ds(handed_at, half)], p_routed.at[block(k)],
            yts_sem.at[i], ytr_sem.at[i],
        ))

    loads[0].wait()
    loads[1].wait()

    @pl.loop(0, slots // ROWS)
    def _(step):
        rows = pl.ds(pl.multiple_of(step * ROWS, ROWS), ROWS)
        x = routed[rows, :]
        g = dot(x, wg[...])
        u = dot(x, wu[...])
        gate_pre[rows, :] = g
        up_pre[rows, :] = u
        acts[2, rows, :] = (g * jax.nn.sigmoid(g) * u).astype(bf16)

    def send_act(j):
        act_to_mate[j] = to_mate(acts.at[j], p_acts.at[j], yas_sem.at[j], yar_sem.at[j])

    send_act(2)

    for position, i in enumerate([0] + order):
        k = lax.rem(me + experts - i, experts)
        if i:
            cot_copies[position - 1].wait_recv()
        weight = cotp[block(k), width:].astype(f32)[:, 0:1]
        scaled[block(k), :] = (weight * cotp[block(k), 0:width].astype(f32)).astype(bf16)
        sca_to_mate.append(to_mate(
            scaled.at[block(k), pl.ds(handed_at, half)], p_scaled.at[block(k)],
            yss_sem.at[i], ysr_sem.at[i],
        ))

    loads[2].wait()

    @pl.loop(0, slots // ROWS)
    def _(step):
        rows = pl.ds(pl.multiple_of(step * ROWS, ROWS), ROWS)
        hg = dot(scaled[rows, :], wd[...], 1, 1)
        g, u = gate_pre[rows, :], up_pre[rows, :]
        s = jax.nn.sigmoid(g)
        acts[1, rows, :] = (hg * (g * s)).astype(bf16)
        acts[0, rows, :] = (hg * u * s * (1.0 + g * (1.0 - s))).astype(bf16)

    send_act(1)
    send_act(0)

    scaling = 1.0 / (experts * cap)
    tot_rows = lax.broadcasted_iota(i32, (8, LANES), 0)

    def steps_of(level):
        return level + 1

    def step_at(grad, level, step):
        return grad * (levels * (levels + 1) // 2) + level * (level + 1) // 2 + step

    tot_copies, x_copies = [], []

    def share(grad, level, step):
        at = step_at(grad, level, step)
        bit = levels - 1 - level + step
        copy = pltpu.make_async_remote_copy(
            tot_send.at[at], tot_recv.at[at], ts_sem.at[at], tr_sem.at[at],
            device_id={"dp": mates[bit]}, device_id_type=MESH,
        )
        copy.start()
        tot_copies.append(copy)
        return copy

    def begin_totals(grad, level, own_sq, part_sq, inner):
        is_former = bits[levels - 1 - level] == 0
        former = jnp.where(is_former, own_sq, part_sq)
        latter = jnp.where(is_former, part_sq, own_sq)
        packed = jnp.where(
            tot_rows == 0, former, jnp.where(tot_rows == 1, latter, inner)
        )
        tot_send[step_at(grad, level, 0)] = packed
        return share(grad, level, 0)

    def end_totals(grad, level, copy):
        for step in range(steps_of(level)):
            at = step_at(grad, level, step)
            copy.wait_recv()
            total = tot_send[at] + tot_recv[at]
            if step + 1 < steps_of(level):
                tot_send[at + 1] = total
                copy = share(grad, level, step + 1)
        former, latter, inner = total[0:1, 0:1], total[1:2, 0:1], total[2:3, 0:1]
        former_coef = 1.0 - inner / (2.0 * (former + epsilon))
        latter_coef = 1.0 - inner / (2.0 * (latter + epsilon))
        is_former = bits[levels - 1 - level] == 0
        return (
            jnp.where(is_former, former_coef, latter_coef),
            jnp.where(is_former, latter_coef, former_coef),
        )

    def whole(partial):
        return jnp.sum(partial, axis=1, keepdims=True)

    def first_level(grad):
        left, p_left = (scaled, p_scaled) if grad == 2 else (routed, p_routed)
        zero = jnp.zeros((1, hidden), f32)

        def body(step, sums):
            here = pl.multiple_of(step * LANES, LANES)
            there = pl.multiple_of(kept_at + step * LANES, LANES)
            a = dot(left[:, pl.ds(there, LANES)], acts[grad], 0, 0) * scaling
            b = dot(p_left[:, pl.ds(here, LANES)], p_acts[grad], 0, 0) * scaling
            own[grad, pl.ds(here, LANES), :] = a
            part[grad, pl.ds(here, LANES), :] = b
            return (
                sums[0] + jnp.sum(a * a, axis=0, keepdims=True),
                sums[1] + jnp.sum(b * b, axis=0, keepdims=True),
                sums[2] + jnp.sum(a * b, axis=0, keepdims=True),
            )

        sums = lax.fori_loop(0, half // LANES, body, (zero, zero, zero))
        return begin_totals(grad, 0, *[whole(s) for s in sums])

    def x_at(grad, level):
        return grad * max(levels - 1, 1) + level - 1

    def hand_over(grad, level, coefs):
        bit = levels - 1 - level
        size = half >> level
        keep_from = pl.multiple_of(bits[bit] * size, LANES)
        hand_from = pl.multiple_of((1 - bits[bit]) * size, LANES)
        sent = handed.at[grad, pl.ds(half - (half >> (level - 1)), size), :]
        at = x_at(grad, level)

        @pl.loop(0, size // LANES)
        def _(step):
            here = pl.multiple_of(step * LANES, LANES)
            theirs = pl.ds(pl.multiple_of(hand_from + step * LANES, LANES), LANES)
            sent[pl.ds(here, LANES), :] = (
                coefs[0] * own[grad, theirs, :] + coefs[1] * part[grad, theirs, :]
            ).astype(bf16)

        copy = pltpu.make_async_remote_copy(
            sent, landed.at[grad, pl.ds(half - (half >> (level - 1)), size), :],
            xs_sem.at[at], xr_sem.at[at], device_id={"dp": mates[bit]}, device_id_type=MESH,
        )
        copy.start()
        x_copies.append(copy)

        @pl.loop(0, size // LANES)
        def _(step):
            here = pl.multiple_of(step * LANES, LANES)
            ours = pl.ds(pl.multiple_of(keep_from + step * LANES, LANES), LANES)
            own[grad, pl.ds(here, LANES), :] = (
                coefs[0] * own[grad, ours, :] + coefs[1] * part[grad, ours, :]
            )

        return copy

    def next_level(grad, level, copy):
        size = half >> level
        start = half - (half >> (level - 1))
        copy.wait_recv()
        zero = jnp.zeros((1, hidden), f32)

        def body(step, sums):
            here = pl.ds(pl.multiple_of(step * LANES, LANES), LANES)
            a = own[grad, here, :]
            b = landed[grad, pl.ds(pl.multiple_of(start + step * LANES, LANES), LANES), :]
            b = b.astype(f32)
            part[grad, here, :] = b
            return (
                sums[0] + jnp.sum(a * a, axis=0, keepdims=True),
                sums[1] + jnp.sum(b * b, axis=0, keepdims=True),
                sums[2] + jnp.sum(a * b, axis=0, keepdims=True),
            )

        sums = lax.fori_loop(0, size // LANES, body, (zero, zero, zero))
        return begin_totals(grad, level, *[whole(s) for s in sums])

    def finish(grad, coefs):
        size = half >> (levels - 1)
        target = (out_gate, out_up, out_down)[grad]

        @pl.loop(0, size // LANES)
        def _(step):
            here = pl.ds(pl.multiple_of(step * LANES, LANES), LANES)
            value = coefs[0] * own[grad, here, :] + coefs[1] * part[grad, here, :]
            if grad == 2:
                target[0, :, here] = value.T
            else:
                target[0, here, :] = value

    for copy in sca_to_mate + tok_to_mate:
        copy.wait_recv()
    act_to_mate[2].wait_recv()
    pending = {2: first_level(2)}

    @pl.loop(0, slots // ROWS)
    def _(step):
        rows = pl.ds(pl.multiple_of(step * ROWS, ROWS), ROWS)
        back = dot(acts[0, rows, :], wg[...], 1, 1) + dot(acts[1, rows, :], wu[...], 1, 1)
        ret_send[rows, 0:width] = back.astype(bf16)
        output = dot(acts[2, rows, :], wd[...])
        score = jnp.sum(output * cotp[rows, 0:width].astype(f32), axis=1, keepdims=True)
        ret_send[rows, width:] = jnp.broadcast_to(score, (ROWS, LANES)).astype(bf16)

    ret_copies = []
    for i in order:
        k = lax.rem(me + i, experts)
        copy = pltpu.make_async_remote_copy(
            ret_send.at[block(k)], ret_recv.at[block(me)], sr_sem.at[i], rr_sem.at[i],
            device_id={"expert": k}, device_id_type=MESH,
        )
        copy.start()
        ret_copies.append(copy)
    ret_recv[block(me), :] = ret_send[block(me), :]

    moving = {}
    for grad in (2, 1, 0):
        if grad != 2:
            act_to_mate[grad].wait_recv()
            pending[grad] = first_level(grad)
        coefs = end_totals(grad, 0, pending[grad])
        if levels > 1:
            moving[grad] = hand_over(grad, 1, coefs)
        else:
            finish(grad, coefs)
    for level in range(1, levels):
        for grad in (2, 1, 0):
            pending[grad] = next_level(grad, level, moving[grad])
            coefs = end_totals(grad, level, pending[grad])
            if level + 1 < levels:
                moving[grad] = hand_over(grad, level + 1, coefs)
            else:
                finish(grad, coefs)

    for copy in ret_copies:
        copy.wait_recv()

    @pl.loop(0, width // 512)
    def _(step):
        columns = pl.ds(pl.multiple_of(step * 512, 512), 512)
        out_in[:, columns] = dot(select[...], ret_recv[:, columns], 0, 0).astype(bf16)

    chosen_by = rout[...]
    scores = jnp.zeros((tokens, chosen_by.shape[1]), f32)
    for k in range(experts):
        rows = slice(k * capp, (k + 1) * capp)
        score = dot(select[rows, :], ret_recv[rows, width:], 0, 0)
        scores = scores + jnp.where(chosen_by == k, score[:, 0 : chosen_by.shape[1]], 0.0)
    out_router[...] = scores.astype(bf16)

    for copy in tok_copies + cot_copies + ret_copies + y_copies + tot_copies + x_copies:
        copy.wait_send()


def per_device(experts, replicas, tokens, routing, probs, cotangent, w_gate, w_up, w_down):
    rows, top = routing.shape
    width = tokens.shape[1]
    hidden = w_gate.shape[2]
    cap = 5 * rows * top // (4 * experts)
    capp = -(-cap // 16) * 16
    slots = experts * capp
    levels = replicas.bit_length() - 1
    half = width // 2
    shard = width // replicas
    steps = 3 * (levels * (levels + 1) // 2)
    wide = width + LANES
    vm, dma = pltpu.VMEM, pltpu.SemaphoreType.DMA
    in_vmem = pl.BlockSpec(memory_space=pltpu.VMEM)
    in_any = pl.BlockSpec(memory_space=pl.ANY)
    names = max(16, experts)
    return tuple(pl.pallas_call(
        functools.partial(kernel, experts, replicas, cap, capp),
        out_shape=(
            jax.ShapeDtypeStruct((1, shard, hidden), f32),
            jax.ShapeDtypeStruct((1, shard, hidden), f32),
            jax.ShapeDtypeStruct((1, hidden, shard), f32),
            jax.ShapeDtypeStruct((rows, width), bf16),
            jax.ShapeDtypeStruct((rows, top), bf16),
        ),
        in_specs=[in_vmem] * 5 + [in_any] * 3,
        out_specs=(in_vmem,) * 5,
        scratch_shapes=[
            vm((width, hidden), bf16), vm((width, hidden), bf16), vm((hidden, width), bf16),
            vm((names, rows), i32), vm((names, rows), f32), vm((slots, rows), bf16),
            vm((slots, width), bf16), vm((slots, wide), bf16),
            vm((slots, width), bf16), vm((slots, wide), bf16), vm((slots, width), bf16),
            vm((slots, hidden), f32), vm((slots, hidden), f32), vm((3, slots, hidden), bf16),
            vm((slots, half), bf16), vm((slots, half), bf16), vm((3, slots, hidden), bf16),
            vm((slots, wide), bf16), vm((slots, wide), bf16),
            vm((3, half, hidden), f32), vm((3, half, hidden), f32),
            vm((3, half, hidden), bf16), vm((3, half, hidden), bf16),
            vm((steps, 8, LANES), f32), vm((steps, 8, LANES), f32),
            dma((3,)),
        ] + [dma((experts,))] * 10 + [dma((3,))] * 2
        + [dma((3 * max(levels - 1, 1),))] * 2 + [dma((steps,))] * 2,
        compiler_params=pltpu.CompilerParams(
            collective_id=0, has_side_effects=True, vmem_limit_bytes=67_000_000
        ),
        name="adasum_moe",
    )(
        tokens, cotangent, routing, routing.T, probs.T.astype(f32), w_gate, w_up, w_down
    ))


def solution(mesh):
    rows = P(("dp", "expert"), None)
    return jax.shard_map(
        functools.partial(per_device, mesh.shape["expert"], mesh.shape["dp"]),
        mesh=mesh,
        in_specs=(rows,) * 4 + (P("expert", None, None),) * 3,
        out_specs=(
            P("expert", "dp", None),
            P("expert", "dp", None),
            P("expert", None, "dp"),
            rows,
            rows,
        ),
        check_vma=False,
    )
```

time: 251 us -> 164 us (0.65); the launches traced: 248 us -> 164 us
  Pallas kernels: 0 us -> 154 us
  waiting for transfers between devices: 88.1 us -> 0 us
  blocking collectives: 50 us -> 0 us
  other arithmetic: 27.5 us -> 1.22 us
  starting transfers between devices: 25.3 us -> 0 us
  local copies, waits for them, and re-layouts: 32.5 us -> 7.95 us
  matrix products: 23.3 us -> 0 us
    pallas_call x0 -> x1, Pallas kernels: none -> 154 us  [per_device(): pl.pallas_call(functools.partial(kernel, experts, replicas, cap, capp), o...]
    ppermute x2 -> x0, waiting for transfers between devices: 49.5 us -> none  [partner_2(): return lax.ppermute(value, axis, pairs)]
    all_to_all x4 -> x0, waiting for transfers between devices: 38.6 us -> none  [the longest x1 22.9 us: per_device(): lax.all_to_all(send_cot.reshape(experts, capacity, model_width), 'expert'...]
    all_to_all x1 -> x0, blocking collectives: 34.9 us -> none  [per_device(): lax.all_to_all(send_rows.reshape(experts, capacity, model_width), 'expert...]
    all_to_all x4 -> x0, starting transfers between devices: 24.2 us -> none  [the longest x1 6.69 us: per_device(): lax.all_to_all(router_slots.reshape(experts, capacity), 'expert', split_a...]
    dot_general x12 -> x0, matrix products: 23.3 us -> none  [the longest x9 14.4 us: contract(): lax.dot_general(former, latter, (((former_dim,), (latter_dim,)), ((), ())...]
    all_gather x2 -> x0, blocking collectives: 15.2 us -> none  [group_totals(): gathered = lax.all_gather(totals[None], 'dp', axis=0, tiled=True)]
    gather x5 -> x0, local copies, waits for them, and re-layouts: 12.7 us -> none  [the longest x1 3.03 us: per_device(): send_rows = jnp.take(tokens, token_of, axis=0, mode='fill', fill_value=0)]
  transfers between devices with their start and end apart: 6 -> 0, of which waited for: 4 -> 0; matrix products, arithmetic and copies ran while one was open for 20% -> 0% of each run, Pallas kernels for 0% -> 0%
where the time goes in v1:
time: 164 us
  Pallas kernels  154 us (94%)
  local copies, waits for them, and re-layouts  7.95 us (5%)
    pallas_call x1, Pallas kernels, per_device(): pl.pallas_call(functools.partial(kernel, experts, replicas, cap, capp), o...  154 us
    unnamed x11, local copies, waits for them, and re-layouts  6.51 us

profile of v1, /device:TPU:12, one launch (start us, length us, event | category | flops | bytes accessed | tf_op | source)
XLA Modules:
  0.0 164.3 jit_solution(17737739682044832653)
XLA Ops:
  0.6 1.2 convert_bitcast_fusion.prob_t
  1.9 1.4 copy.12.rout
  3.3 154.4 %adasum_moe.1 = (f32[1,512,512]{2,1,0:T(8,128)}, f32[1,512,512]{2,1,0:T(8,128)}, f32[1,512,512]{2,1,0:T(8,128)}, bf16[128,2048]{1,0:T(8,128)(2,1)}, bf16[128,2]{1,0:T(8,128)(2,1)}) custom-call(bf16[128,2048]{1,0:T(8,128)(2,1)} %tok.1, bf16[128,2048]{1,0:T(8,128)(2,1)} %cot.1, s32[128,2]{1,0:T(8,128)} %copy.12.rout, s32[2,128]{1,0:T(2,128)} %bitcast.3, ...), custom_call_target="tpu_custom_call" | custom-call | tf_op jit(solution)/shard_map/adasum_moe/pallas_call | solution.py:402
  157.7 0.0 copy-start.1
  157.7 1.4 copy.13
  159.2 0.0 copy-start
  159.2 2.4 %copy.18 = f32[1,512,512]{2,1,0:T(8,128)} copy(f32[1,512,512]{2,1,0:T(8,128)} %get-tuple-element.15) | data formatting | bytes 2097152
  161.5 0.0 copy-done.1
  161.5 0.0 copy-start.2
  161.5 1.0 copy.19
  162.5 0.0 copy-done
  162.5 1.0 copy.20
  163.5 0.0 copy-done.2
  163.5 0.8 copy.21
Async XLA Ops:
  157.7 3.8 %copy-start.1 = (f32[1,512,512]{2,1,0:T(8,128)S(1)}, f32[1,512,512]{2,1,0:T(8,128)}, u32[]{:S(2)}) copy-start(f32[1,512,512]{2,1,0:T(8,128)} %get-tuple-element.16) | copy-start | bytes 3145732
  159.2 3.3 %copy-start = (f32[1,512,512]{2,1,0:T(8,128)S(1)}, f32[1,512,512]{2,1,0:T(8,128)}, u32[]{:S(2)}) copy-start(f32[1,512,512]{2,1,0:T(8,128)} %get-tuple-element.17) | copy-start | bytes 3145732
  161.5 1.9 %copy-start.2 = (bf16[128,2048]{1,0:T(8,128)(2,1)S(1)}, bf16[128,2048]{1,0:T(8,128)(2,1)}, u32[]{:S(2)}) copy-start(bf16[128,2048]{1,0:T(8,128)(2,1)} %get-tuple-element.18) | copy-start | bytes 1572868

commit v2 on v1

--- a/solution.py
+++ b/solution.py
@@ -18,7 +18,7 @@
     return lax.dot_general(a, b, (((ad,), (bd,)), ((), ())), preferred_element_type=f32)
 
 
-def kernel(
+def halving_kernel(
     experts, replicas, cap, capp,
     tok, cot, rout, rout_t, prob_t, wg_hbm, wu_hbm, wd_hbm,
     out_gate, out_up, out_down, out_in, out_router,
@@ -383,6 +383,325 @@
         copy.wait_send()
 
 
+def kernel(
+    experts, replicas, cap, capp,
+    tok, cot, rout, rout_t, prob_t, wg_hbm, wu_hbm, wd_hbm,
+    out_gate, out_up, out_down, out_in, out_router,
+    wg, wu, wd, ranks, weights, select, send_tok, send_cot, routed, cotp, scaled,
+    gate_pre, up_pre, acts, p_routed, p_scaled, p_acts, ret_send, ret_recv,
+    grads, gram_send, gram_recv,
+    w_sem, st_sem, rt_sem, sc_sem, rc_sem, sr_sem, rr_sem,
+    yts_sem, ytr_sem, yss_sem, ysr_sem, yas_sem, yar_sem, gs_sem, gr_sem,
+):
+    me = lax.axis_index("expert")
+    dp = lax.axis_index("dp")
+    tokens, width = tok.shape
+    hidden = wg.shape[1]
+    slots = experts * capp
+    levels = replicas.bit_length() - 1
+    quarter = width // replicas
+    bits = [lax.rem(dp // (1 << b), 2) for b in range(levels)]
+    mates = [
+        dp + sum((1 << b) * (1 - 2 * bits[b]) for b in range(levels) if j >> b & 1)
+        for j in range(replicas)
+    ]
+    others = range(1, replicas)
+    order = sorted(range(1, experts), key=lambda i: abs(2 * i - experts))
+
+    def block(index):
+        return pl.ds(pl.multiple_of(index * capp, capp), capp)
+
+    loads = [
+        pltpu.make_async_copy(src.at[0], dst, w_sem.at[j])
+        for j, (src, dst) in enumerate(((wg_hbm, wg), (wu_hbm, wu), (wd_hbm, wd)))
+    ]
+    for load in loads:
+        load.start()
+
+    barrier = pltpu.get_barrier_semaphore()
+    for i in range(1, experts):
+        pl.semaphore_signal(
+            barrier, inc=1, device_id={"expert": lax.rem(me + i, experts)}, device_id_type=MESH
+        )
+    for mate in mates[1:]:
+        pl.semaphore_signal(barrier, inc=1, device_id={"dp": mate}, device_id_type=MESH)
+
+    first, second = rout_t[0:1, :], rout_t[1:2, :]
+    names = lax.broadcasted_iota(i32, ranks.shape, 0)
+    is_first, is_second = names == first, names == second
+    member = jnp.where(is_first | is_second, 1.0, 0.0).astype(f32)
+    earlier = lax.broadcasted_iota(i32, (tokens, tokens), 0)
+    later = lax.broadcasted_iota(i32, (tokens, tokens), 1)
+    before = dot(member.astype(bf16), jnp.where(earlier < later, 1.0, 0.0).astype(bf16))
+    ranks[...] = jnp.where(member > 0.0, before, -1.0).astype(i32)
+    weights[...] = jnp.where(
+        is_first, prob_t[0:1, :], jnp.where(is_second, prob_t[1:2, :], 0.0)
+    )
+    slot = lax.broadcasted_iota(i32, (capp, tokens), 0)
+
+    def picks(expert):
+        return slot == ranks[pl.ds(expert, 1), :]
+
+    pl.semaphore_wait(barrier, experts + replicas - 2)
+
+    tok_copies, cot_copies = [], []
+    for i in order:
+        k = lax.rem(me + i, experts)
+        chosen = jnp.where(picks(k), 1.0, 0.0).astype(bf16)
+        select[block(k), :] = chosen
+        send_tok[block(k), :] = dot(chosen, tok[...]).astype(bf16)
+        copy = pltpu.make_async_remote_copy(
+            send_tok.at[block(k)], routed.at[block(me)], st_sem.at[i], rt_sem.at[i],
+            device_id={"expert": k}, device_id_type=MESH,
+        )
+        copy.start()
+        tok_copies.append(copy)
+
+    def fill_cot(target, k):
+        picked = picks(k)
+        chosen = jnp.where(picked, 1.0, 0.0).astype(bf16)
+        weight = jnp.sum(
+            jnp.where(picked, weights[pl.ds(k, 1), :], 0.0), axis=1, keepdims=True
+        )
+        target[block(k), 0:width] = dot(chosen, cot[...]).astype(bf16)
+        target[block(k), width:] = jnp.broadcast_to(weight, (capp, LANES)).astype(bf16)
+        return chosen
+
+    for i in order:
+        k = lax.rem(me + i, experts)
+        fill_cot(send_cot, k)
+        copy = pltpu.make_async_remote_copy(
+            send_cot.at[block(k)], cotp.at[block(me)], sc_sem.at[i], rc_sem.at[i],
+            device_id={"expert": k}, device_id_type=MESH,
+        )
+        copy.start()
+        cot_copies.append(copy)
+    mine = fill_cot(cotp, me)
+    select[block(me), :] = mine
+    routed[block(me), :] = dot(mine, tok[...]).astype(bf16)
+
+    y_copies = []
+
+    def columns_of(mate):
+        return pl.ds(pl.multiple_of(mate * quarter, LANES), quarter)
+
+    def to_mate(j, source, target, send_sem, recv_sem):
+        copy = pltpu.make_async_remote_copy(
+            source, target, send_sem, recv_sem, device_id={"dp": mates[j]}, device_id_type=MESH
+        )
+        copy.start()
+        y_copies.append(copy)
+        return copy
+
+    tok_to_mate, sca_to_mate, act_to_mate = [], [], {}
+    for position, i in enumerate([0] + order):
+        k = lax.rem(me + experts - i, experts)
+        if i:
+            tok_copies[position - 1].wait_recv()
+        for j in others:
+            tok_to_mate.append(to_mate(
+                j, routed.at[block(k), columns_of(mates[j])], p_routed.at[j, block(k)],
+                yts_sem.at[j, i], ytr_sem.at[j, i],
+            ))
+
+    loads[0].wait()
+    loads[1].wait()
+
+    @pl.loop(0, slots // ROWS)
+    def _(step):
+        rows = pl.ds(pl.multiple_of(step * ROWS, ROWS), ROWS)
+        x = routed[rows, :]
+        g = dot(x, wg[...])
+        u = dot(x, wu[...])
+        gate_pre[rows, :] = g
+        up_pre[rows, :] = u
+        acts[2, rows, :] = (g * jax.nn.sigmoid(g) * u).astype(bf16)
+
+    def send_act(grad, j, source=None):
+        act_to_mate[grad, source or j] = to_mate(
+            j, p_acts.at[grad, source ^ j] if source else acts.at[grad],
+            p_acts.at[grad, source or j],
+            yas_sem.at[grad, source or j], yar_sem.at[grad, source or j],
+        )
+
+    for j in others:
+        send_act(2, j)
+
+    for position, i in enumerate([0] + order):
+        k = lax.rem(me + experts - i, experts)
+        if i:
+            cot_copies[position - 1].wait_recv()
+        weight = cotp[block(k), width:].astype(f32)[:, 0:1]
+        scaled[block(k), :] = (weight * cotp[block(k), 0:width].astype(f32)).astype(bf16)
+        for j in others:
+            sca_to_mate.append(to_mate(
+                j, scaled.at[block(k), columns_of(mates[j])], p_scaled.at[j, block(k)],
+                yss_sem.at[j, i], ysr_sem.at[j, i],
+            ))
+
+    loads[2].wait()
+
+    @pl.loop(0, slots // ROWS)
+    def _(step):
+        rows = pl.ds(pl.multiple_of(step * ROWS, ROWS), ROWS)
+        hg = dot(scaled[rows, :], wd[...], 1, 1)
+        g, u = gate_pre[rows, :], up_pre[rows, :]
+        s = jax.nn.sigmoid(g)
+        acts[1, rows, :] = (hg * (g * s)).astype(bf16)
+        acts[0, rows, :] = (hg * u * s * (1.0 + g * (1.0 - s))).astype(bf16)
+
+    relayed = replicas == 4
+    near = (1, 2) if relayed else others
+    for grad in (1, 0):
+        for j in near:
+            send_act(grad, j)
+
+    scaling = 1.0 / (experts * cap)
+    pairs = [(i, j) for i in range(replicas) for j in range(i, replicas)]
+
+    def grad_of(grad, j):
+        left, p_left = (scaled, p_scaled) if grad == 2 else (routed, p_routed)
+
+        @pl.loop(0, quarter // LANES)
+        def _(step):
+            here = pl.ds(pl.multiple_of(step * LANES, LANES), LANES)
+            if j:
+                x, y = p_left[j, :, here], p_acts[grad, j]
+            else:
+                there = pl.multiple_of(dp * quarter + step * LANES, LANES)
+                x, y = left[:, pl.ds(there, LANES)], acts[grad]
+            grads[grad, j, here, :] = dot(x, y, 0, 0) * scaling
+
+    def gram_of(grad):
+        def body(step, sums):
+            here = pl.ds(pl.multiple_of(step * 8, 8), 8)
+            held = [grads[grad, j, here, :] for j in range(replicas)]
+            return tuple(s + held[i] * held[j] for s, (i, j) in zip(sums, pairs))
+
+        zero = jnp.zeros((8, hidden), f32)
+        sums = lax.fori_loop(0, quarter // 8, body, (zero,) * len(pairs))
+        for row, total in enumerate(sums):
+            total = jnp.sum(jnp.sum(total, axis=0, keepdims=True), axis=1, keepdims=True)
+            gram_send[grad, row : row + 1, :] = jnp.broadcast_to(total, (1, LANES))
+
+    def combine(grad):
+        def entry(i, j):
+            total = 0.0
+            for m in range(replicas):
+                row = pairs.index(tuple(sorted((i ^ m, j ^ m))))
+                held = gram_recv[m, grad, row : row + 1, :] if m else gram_send[grad, row : row + 1, :]
+                total = total + held
+            return total
+
+        gram = {pair: entry(*pair) for pair in pairs}
+
+        def product(left, right):
+            return sum(
+                left[i] * right[j] * gram[min(i, j), max(i, j)] for i in left for j in right
+            )
+
+        vectors = [{j: jnp.ones((1, LANES), f32)} for j in range(replicas)]
+        while len(vectors) > 1:
+            count = len(vectors) // 2
+            joined = []
+            for j in range(count):
+                a, b = vectors[j], vectors[j + count]
+                inner = product(a, b)
+                na = jnp.maximum(product(a, a), 0.0)
+                nb = jnp.maximum(product(b, b), 0.0)
+                ca = 1.0 - inner / (2.0 * (na + epsilon))
+                cb = 1.0 - inner / (2.0 * (nb + epsilon))
+                joined.append({
+                    **{i: ca * c for i, c in a.items()}, **{i: cb * c for i, c in b.items()}
+                })
+            vectors = joined
+        coefs = [vectors[0][j][:, 0:1] for j in range(replicas)]
+        target = (out_gate, out_up, out_down)[grad]
+
+        @pl.loop(0, quarter // LANES)
+        def _(step):
+            here = pl.ds(pl.multiple_of(step * LANES, LANES), LANES)
+            value = coefs[0] * grads[grad, 0, here, :]
+            for j in others:
+                value = value + coefs[j] * grads[grad, j, here, :]
+            if grad == 2:
+                target[0, :, here] = value.T
+            else:
+                target[0, here, :] = value
+
+    @pl.loop(0, slots // ROWS)
+    def _(step):
+        rows = pl.ds(pl.multiple_of(step * ROWS, ROWS), ROWS)
+        back = dot(acts[0, rows, :], wg[...], 1, 1) + dot(acts[1, rows, :], wu[...], 1, 1)
+        ret_send[rows, 0:width] = back.astype(bf16)
+        output = dot(acts[2, rows, :], wd[...])
+        score = jnp.sum(output * cotp[rows, 0:width].astype(f32), axis=1, keepdims=True)
+        ret_send[rows, width:] = jnp.broadcast_to(score, (ROWS, LANES)).astype(bf16)
+
+    ret_copies = []
+    for i in order:
+        k = lax.rem(me + i, experts)
+        copy = pltpu.make_async_remote_copy(
+            ret_send.at[block(k)], ret_recv.at[block(me)], sr_sem.at[i], rr_sem.at[i],
+            device_id={"expert": k}, device_id_type=MESH,
+        )
+        copy.start()
+        ret_copies.append(copy)
+    ret_recv[block(me), :] = ret_send[block(me), :]
+
+    for copy in sca_to_mate + tok_to_mate:
+        copy.wait_recv()
+    for grad in (2, 1, 0):
+        grad_of(grad, 0)
+    for j in others:
+        act_to_mate[2, j].wait_recv()
+        grad_of(2, j)
+    gram_of(2)
+    for grad, far in ((1, 1), (0, 2)):
+        for j in near:
+            act_to_mate[grad, j].wait_recv()
+        if relayed:
+            send_act(grad, far, 3)
+        for j in near:
+            grad_of(grad, j)
+    for grad in (1, 0):
+        if relayed:
+            act_to_mate[grad, 3].wait_recv()
+            grad_of(grad, 3)
+        gram_of(grad)
+    gram_copies = []
+    for j in others:
+        copy = pltpu.make_async_remote_copy(
+            gram_send, gram_recv.at[j], gs_sem.at[j], gr_sem.at[j],
+            device_id={"dp": mates[j]}, device_id_type=MESH,
+        )
+        copy.start()
+        gram_copies.append(copy)
+    for copy in gram_copies:
+        copy.wait_recv()
+    for grad in (2, 1, 0):
+        combine(grad)
+
+    for copy in ret_copies:
+        copy.wait_recv()
+
+    @pl.loop(0, width // 512)
+    def _(step):
+        columns = pl.ds(pl.multiple_of(step * 512, 512), 512)
+        out_in[:, columns] = dot(select[...], ret_recv[:, columns], 0, 0).astype(bf16)
+
+    chosen_by = rout[...]
+    scores = jnp.zeros((tokens, chosen_by.shape[1]), f32)
+    for k in range(experts):
+        rows = slice(k * capp, (k + 1) * capp)
+        score = dot(select[rows, :], ret_recv[rows, width:], 0, 0)
+        scores = scores + jnp.where(chosen_by == k, score[:, 0 : chosen_by.shape[1]], 0.0)
+    out_router[...] = scores.astype(bf16)
+
+    for copy in tok_copies + cot_copies + ret_copies + y_copies + gram_copies:
+        copy.wait_send()
+
+
 def per_device(experts, replicas, tokens, routing, probs, cotangent, w_gate, w_up, w_down):
     rows, top = routing.shape
     width = tokens.shape[1]
@@ -393,14 +712,16 @@
     levels = replicas.bit_length() - 1
     half = width // 2
     shard = width // replicas
+    direct = replicas <= 4
     steps = 3 * (levels * (levels + 1) // 2)
     wide = width + LANES
     vm, dma = pltpu.VMEM, pltpu.SemaphoreType.DMA
     in_vmem = pl.BlockSpec(memory_space=pltpu.VMEM)
     in_any = pl.BlockSpec(memory_space=pl.ANY)
     names = max(16, experts)
+    grams = -(-replicas * (replicas + 1) // 16) * 8
     return tuple(pl.pallas_call(
-        functools.partial(kernel, experts, replicas, cap, capp),
+        functools.partial(kernel if direct else halving_kernel, experts, replicas, cap, capp),
         out_shape=(
             jax.ShapeDtypeStruct((1, shard, hidden), f32),
             jax.ShapeDtypeStruct((1, shard, hidden), f32),
@@ -416,14 +737,26 @@
             vm((slots, width), bf16), vm((slots, wide), bf16),
             vm((slots, width), bf16), vm((slots, wide), bf16), vm((slots, width), bf16),
             vm((slots, hidden), f32), vm((slots, hidden), f32), vm((3, slots, hidden), bf16),
+        ] + ([
+            vm((replicas, slots, shard), bf16), vm((replicas, slots, shard), bf16),
+            vm((3, replicas, slots, hidden), bf16),
+        ] if direct else [
             vm((slots, half), bf16), vm((slots, half), bf16), vm((3, slots, hidden), bf16),
+        ]) + [
             vm((slots, wide), bf16), vm((slots, wide), bf16),
+        ] + ([
+            vm((3, replicas, shard, hidden), f32),
+            vm((3, grams, LANES), f32), vm((replicas, 3, grams, LANES), f32),
+        ] if direct else [
             vm((3, half, hidden), f32), vm((3, half, hidden), f32),
             vm((3, half, hidden), bf16), vm((3, half, hidden), bf16),
             vm((steps, 8, LANES), f32), vm((steps, 8, LANES), f32),
-            dma((3,)),
-        ] + [dma((experts,))] * 10 + [dma((3,))] * 2
-        + [dma((3 * max(levels - 1, 1),))] * 2 + [dma((steps,))] * 2,
+        ]) + [dma((3,))] + [dma((experts,))] * 6 + ([
+            dma((replicas, experts)), dma((replicas, experts)),
+            dma((replicas, experts)), dma((replicas, experts)),
+            dma((3, replicas)), dma((3, replicas)), dma((replicas,)), dma((replicas,)),
+        ] if direct else [dma((experts,))] * 4 + [dma((3,))] * 2
+            + [dma((3 * max(levels - 1, 1),))] * 2 + [dma((steps,))] * 2),
         compiler_params=pltpu.CompilerParams(
             collective_id=0, has_side_effects=True, vmem_limit_bytes=67_000_000
         ),

time: 164 us -> 146 us (0.89); the launches traced: 164 us -> 143 us
  Pallas kernels: 154 us -> 133 us
    pallas_call x1, Pallas kernels: 154 us -> 133 us  [per_device(): pl.pallas_call(functools.partial(kernel if direct else halving_kernel, ex...]
where the time goes in v2:
time: 146 us; the launch traced here: 143 us
  Pallas kernels  133 us (91%)
  local copies, waits for them, and re-layouts  7.95 us (5%)
    pallas_call x1, Pallas kernels, per_device(): pl.pallas_call(functools.partial(kernel if direct else halving_kernel, ex...  133 us
    unnamed x11, local copies, waits for them, and re-layouts  6.51 us

profile of v2, /device:TPU:12, one launch (start us, length us, event | category | flops | bytes accessed | tf_op | source)
XLA Modules:
  0.0 143.3 jit_solution(17943365886203881115)
XLA Ops:
  0.6 1.2 convert_bitcast_fusion.prob_t
  1.9 1.4 copy.12.rout
  3.3 133.5 %adasum_moe.1 = (f32[1,512,512]{2,1,0:T(8,128)}, f32[1,512,512]{2,1,0:T(8,128)}, f32[1,512,512]{2,1,0:T(8,128)}, bf16[128,2048]{1,0:T(8,128)(2,1)}, bf16[128,2]{1,0:T(8,128)(2,1)}) custom-call(bf16[128,2048]{1,0:T(8,128)(2,1)} %tok.1, bf16[128,2048]{1,0:T(8,128)(2,1)} %cot.1, s32[128,2]{1,0:T(8,128)} %copy.12.rout, s32[2,128]{1,0:T(2,128)} %bitcast.3, ...), custom_call_target="tpu_custom_call" | custom-call | tf_op jit(solution)/shard_map/adasum_moe/pallas_call | solution.py:723
  136.7 0.0 copy-start.1
  136.7 1.4 %copy.13 = bf16[128,2]{0,1:T(2,128)(2,1)} copy(bf16[128,2]{1,0:T(8,128)(2,1)} %get-tuple-element.9) | data formatting | bytes 1024 | tf_op jit(solution)/shard_map/adasum_moe/pallas_call | solution.py:723
  138.2 0.0 copy-start
  138.2 2.4 %copy.18 = f32[1,512,512]{2,1,0:T(8,128)} copy(f32[1,512,512]{2,1,0:T(8,128)} %get-tuple-element.15) | data formatting | bytes 2097152
  140.5 0.0 copy-done.1
  140.5 0.0 copy-start.2
  140.5 1.0 copy.19
  141.5 0.0 copy-done
  141.5 1.0 copy.20
  142.5 0.0 copy-done.2
  142.5 0.8 copy.21
Async XLA Ops:
  136.7 3.8 %copy-start.1 = (f32[1,512,512]{2,1,0:T(8,128)S(1)}, f32[1,512,512]{2,1,0:T(8,128)}, u32[]{:S(2)}) copy-start(f32[1,512,512]{2,1,0:T(8,128)} %get-tuple-element.16) | copy-start | bytes 3145732
  138.2 3.3 %copy-start = (f32[1,512,512]{2,1,0:T(8,128)S(1)}, f32[1,512,512]{2,1,0:T(8,128)}, u32[]{:S(2)}) copy-start(f32[1,512,512]{2,1,0:T(8,128)} %get-tuple-element.17) | copy-start | bytes 3145732
  140.5 1.9 %copy-start.2 = (bf16[128,2048]{1,0:T(8,128)(2,1)S(1)}, bf16[128,2048]{1,0:T(8,128)(2,1)}, u32[]{:S(2)}) copy-start(bf16[128,2048]{1,0:T(8,128)(2,1)} %get-tuple-element.18) | copy-start | bytes 1572868

commit v3 on v2

--- a/solution.py
+++ b/solution.py
@@ -387,11 +387,11 @@
     experts, replicas, cap, capp,
     tok, cot, rout, rout_t, prob_t, wg_hbm, wu_hbm, wd_hbm,
     out_gate, out_up, out_down, out_in, out_router,
-    wg, wu, wd, ranks, weights, select, send_tok, send_cot, routed, cotp, scaled,
+    wg, wu, wd, ranks, weights, select, send_tok, send_cot, got_tok, got_cot, routed, cotp, scaled,
     gate_pre, up_pre, acts, p_routed, p_scaled, p_acts, ret_send, ret_recv,
     grads, gram_send, gram_recv,
     w_sem, st_sem, rt_sem, sc_sem, rc_sem, sr_sem, rr_sem,
-    yts_sem, ytr_sem, yss_sem, ysr_sem, yas_sem, yar_sem, gs_sem, gr_sem,
+    yts_sem, ytr_sem, yss_sem, ysr_sem, yas_sem, yar_sem, gs_sem, gr_sem, kts_sem, ktr_sem, kcs_sem, kcr_sem,
 ):
     me = lax.axis_index("expert")
     dp = lax.axis_index("dp")
@@ -407,6 +407,12 @@
     ]
     others = range(1, replicas)
     order = sorted(range(1, experts), key=lambda i: abs(2 * i - experts))
+    chips = experts // 2
+    here_chip, core = me // 2, lax.rem(me, 2)
+    sibling = me + 1 - 2 * core
+    both = -(-2 * cap // 16) * 16
+    offset, shift = cap // 16 * 16, cap % 16
+    chip_order = sorted(range(1, chips), key=lambda i: abs(2 * i - chips))
 
     def block(index):
         return pl.ds(pl.multiple_of(index * capp, capp), capp)
@@ -433,52 +439,69 @@
     earlier = lax.broadcasted_iota(i32, (tokens, tokens), 0)
     later = lax.broadcasted_iota(i32, (tokens, tokens), 1)
     before = dot(member.astype(bf16), jnp.where(earlier < later, 1.0, 0.0).astype(bf16))
-    ranks[...] = jnp.where(member > 0.0, before, -1.0).astype(i32)
+    ranks[...] = jnp.where(member > 0.0, before, -1024.0).astype(i32)
     weights[...] = jnp.where(
         is_first, prob_t[0:1, :], jnp.where(is_second, prob_t[1:2, :], 0.0)
     )
     slot = lax.broadcasted_iota(i32, (capp, tokens), 0)
-
-    def picks(expert):
-        return slot == ranks[pl.ds(expert, 1), :]
+    both_slot = lax.broadcasted_iota(i32, (both, tokens), 0)
+
+    def pair(chip):
+        return pl.ds(pl.multiple_of(chip * both, 16), both)
+
+    def window(chip, which):
+        return pl.ds(pl.multiple_of(chip * both + which * offset, 16), capp)
+
+    def fill_tok(target, chip):
+        low = both_slot == ranks[pl.ds(2 * chip, 1), :]
+        high = both_slot == cap + ranks[pl.ds(2 * chip + 1, 1), :]
+        chosen = jnp.where(low | high, 1.0, 0.0).astype(bf16)
+        target[pair(chip), :] = dot(chosen, tok[...]).astype(bf16)
+
+    def fill_cot(target, chip):
+        low = both_slot == ranks[pl.ds(2 * chip, 1), :]
+        high = both_slot == cap + ranks[pl.ds(2 * chip + 1, 1), :]
+        chosen = jnp.where(low | high, 1.0, 0.0).astype(bf16)
+        held = jnp.where(low, weights[pl.ds(2 * chip, 1), :], 0.0)
+        held = jnp.where(high, weights[pl.ds(2 * chip + 1, 1), :], held)
+        weight = jnp.sum(held, axis=1, keepdims=True)
+        target[pair(chip), 0:width] = dot(chosen, cot[...]).astype(bf16)
+        target[pair(chip), width:] = jnp.broadcast_to(weight, (both, LANES)).astype(bf16)
 
     pl.semaphore_wait(barrier, experts + replicas - 2)
 
     tok_copies, cot_copies = [], []
-    for i in order:
-        k = lax.rem(me + i, experts)
-        chosen = jnp.where(picks(k), 1.0, 0.0).astype(bf16)
-        select[block(k), :] = chosen
-        send_tok[block(k), :] = dot(chosen, tok[...]).astype(bf16)
-        copy = pltpu.make_async_remote_copy(
-            send_tok.at[block(k)], routed.at[block(me)], st_sem.at[i], rt_sem.at[i],
-            device_id={"expert": k}, device_id_type=MESH,
-        )
-        copy.start()
-        tok_copies.append(copy)
-
-    def fill_cot(target, k):
-        picked = picks(k)
-        chosen = jnp.where(picked, 1.0, 0.0).astype(bf16)
-        weight = jnp.sum(
-            jnp.where(picked, weights[pl.ds(k, 1), :], 0.0), axis=1, keepdims=True
-        )
-        target[block(k), 0:width] = dot(chosen, cot[...]).astype(bf16)
-        target[block(k), width:] = jnp.broadcast_to(weight, (capp, LANES)).astype(bf16)
-        return chosen
-
-    for i in order:
-        k = lax.rem(me + i, experts)
-        fill_cot(send_cot, k)
-        copy = pltpu.make_async_remote_copy(
-            send_cot.at[block(k)], cotp.at[block(me)], sc_sem.at[i], rc_sem.at[i],
-            device_id={"expert": k}, device_id_type=MESH,
-        )
-        copy.start()
-        cot_copies.append(copy)
-    mine = fill_cot(cotp, me)
-    select[block(me), :] = mine
-    routed[block(me), :] = dot(mine, tok[...]).astype(bf16)
+    def to_chip(i, source, target, send_sem, recv_sem):
+        chip = lax.rem(here_chip + i, chips)
+        copy = pltpu.make_async_remote_copy(
+            source.at[pair(chip)], target.at[pair(here_chip)], send_sem.at[i], recv_sem.at[i],
+            device_id={"expert": 2 * chip + core}, device_id_type=MESH,
+        )
+        copy.start()
+        return copy
+
+    for i in chip_order:
+        fill_tok(send_tok, lax.rem(here_chip + i, chips))
+        tok_copies.append(to_chip(i, send_tok, got_tok, st_sem, rt_sem))
+    for i in chip_order:
+        fill_cot(send_cot, lax.rem(here_chip + i, chips))
+        cot_copies.append(to_chip(i, send_cot, got_cot, sc_sem, rc_sem))
+    fill_tok(got_tok, here_chip)
+    fill_cot(got_cot, here_chip)
+    for k in range(experts):
+        picked = slot == ranks[k : k + 1, :] + k % 2 * shift
+        select[k * capp : (k + 1) * capp, :] = jnp.where(picked, 1.0, 0.0).astype(bf16)
+
+    core_copies = []
+
+    def to_sibling(chip, i, source, target, send_sem, recv_sem):
+        copy = pltpu.make_async_remote_copy(
+            source.at[window(chip, 1 - core)], target.at[block(2 * chip + core)],
+            send_sem.at[i], recv_sem.at[i], device_id={"expert": sibling}, device_id_type=MESH,
+        )
+        copy.start()
+        core_copies.append(copy)
+        return copy
 
     y_copies = []
 
@@ -494,15 +517,29 @@
         return copy
 
     tok_to_mate, sca_to_mate, act_to_mate = [], [], {}
-    for position, i in enumerate([0] + order):
-        k = lax.rem(me + experts - i, experts)
+    def spread_tok(which, i):
+        for j in others:
+            tok_to_mate.append(to_mate(
+                j, routed.at[block(which), columns_of(mates[j])], p_routed.at[j, block(which)],
+                yts_sem.at[j, i], ytr_sem.at[j, i],
+            ))
+
+    def from_sibling(chip, i, copy):
+        copy.wait_recv()
+        spread_tok(2 * chip + 1 - core, 2 * i + 1)
+
+    last = None
+    for position, i in enumerate([0] + chip_order):
+        chip = lax.rem(here_chip + chips - i, chips)
         if i:
             tok_copies[position - 1].wait_recv()
-        for j in others:
-            tok_to_mate.append(to_mate(
-                j, routed.at[block(k), columns_of(mates[j])], p_routed.at[j, block(k)],
-                yts_sem.at[j, i], ytr_sem.at[j, i],
-            ))
+        copy = to_sibling(chip, i, got_tok, routed, kts_sem, ktr_sem)
+        routed[block(2 * chip + core), :] = got_tok[window(chip, core), :]
+        if last:
+            from_sibling(*last)
+        spread_tok(2 * chip + core, 2 * i)
+        last = (chip, i, copy)
+    from_sibling(*last)
 
     loads[0].wait()
     loads[1].wait()
@@ -527,17 +564,36 @@
     for j in others:
         send_act(2, j)
 
-    for position, i in enumerate([0] + order):
-        k = lax.rem(me + experts - i, experts)
+    line = lax.broadcasted_iota(i32, (capp, 1), 0)
+    valid = (line >= core * shift) & (line < core * shift + cap)
+
+    def spread_cot(which, i):
+        weight = jnp.where(valid, cotp[block(which), width:].astype(f32)[:, 0:1], 0.0)
+        scaled[block(which), :] = (
+            weight * cotp[block(which), 0:width].astype(f32)
+        ).astype(bf16)
+        for j in others:
+            sca_to_mate.append(to_mate(
+                j, scaled.at[block(which), columns_of(mates[j])], p_scaled.at[j, block(which)],
+                yss_sem.at[j, i], ysr_sem.at[j, i],
+            ))
+
+    def cot_from_sibling(chip, i, copy):
+        copy.wait_recv()
+        spread_cot(2 * chip + 1 - core, 2 * i + 1)
+
+    last = None
+    for position, i in enumerate([0] + chip_order):
+        chip = lax.rem(here_chip + chips - i, chips)
         if i:
             cot_copies[position - 1].wait_recv()
-        weight = cotp[block(k), width:].astype(f32)[:, 0:1]
-        scaled[block(k), :] = (weight * cotp[block(k), 0:width].astype(f32)).astype(bf16)
-        for j in others:
-            sca_to_mate.append(to_mate(
-                j, scaled.at[block(k), columns_of(mates[j])], p_scaled.at[j, block(k)],
-                yss_sem.at[j, i], ysr_sem.at[j, i],
-            ))
+        copy = to_sibling(chip, i, got_cot, cotp, kcs_sem, kcr_sem)
+        cotp[block(2 * chip + core), :] = got_cot[window(chip, core), :]
+        if last:
+            cot_from_sibling(*last)
+        spread_cot(2 * chip + core, 2 * i)
+        last = (chip, i, copy)
+    cot_from_sibling(*last)
 
     loads[2].wait()
 
@@ -698,7 +754,7 @@
         scores = scores + jnp.where(chosen_by == k, score[:, 0 : chosen_by.shape[1]], 0.0)
     out_router[...] = scores.astype(bf16)
 
-    for copy in tok_copies + cot_copies + ret_copies + y_copies + gram_copies:
+    for copy in tok_copies + cot_copies + ret_copies + y_copies + gram_copies + core_copies:
         copy.wait_send()
 
 
@@ -718,6 +774,7 @@
     vm, dma = pltpu.VMEM, pltpu.SemaphoreType.DMA
     in_vmem = pl.BlockSpec(memory_space=pltpu.VMEM)
     in_any = pl.BlockSpec(memory_space=pl.ANY)
+    paired = experts // 2 * (-(-2 * cap // 16) * 16)
     names = max(16, experts)
     grams = -(-replicas * (replicas + 1) // 16) * 8
     return tuple(pl.pallas_call(
@@ -734,7 +791,12 @@
         scratch_shapes=[
             vm((width, hidden), bf16), vm((width, hidden), bf16), vm((hidden, width), bf16),
             vm((names, rows), i32), vm((names, rows), f32), vm((slots, rows), bf16),
+        ] + ([
+            vm((paired, width), bf16), vm((paired, wide), bf16),
+            vm((paired, width), bf16), vm((paired, wide), bf16),
+        ] if direct else [
             vm((slots, width), bf16), vm((slots, wide), bf16),
+        ]) + [
             vm((slots, width), bf16), vm((slots, wide), bf16), vm((slots, width), bf16),
             vm((slots, hidden), f32), vm((slots, hidden), f32), vm((3, slots, hidden), bf16),
         ] + ([
@@ -755,6 +817,7 @@
             dma((replicas, experts)), dma((replicas, experts)),
             dma((replicas, experts)), dma((replicas, experts)),
             dma((3, replicas)), dma((3, replicas)), dma((replicas,)), dma((replicas,)),
+            dma((experts // 2,)), dma((experts // 2,)), dma((experts // 2,)), dma((experts // 2,)),
         ] if direct else [dma((experts,))] * 4 + [dma((3,))] * 2
             + [dma((3 * max(levels - 1, 1),))] * 2 + [dma((steps,))] * 2),
         compiler_params=pltpu.CompilerParams(

time: 146 us -> 142 us (0.973); the launches traced: 143 us -> 141 us
  Pallas kernels: 133 us -> 131 us
    pallas_call x1, Pallas kernels: 133 us -> 131 us  [per_device(): pl.pallas_call(functools.partial(kernel if direct else halving_kernel, ex...]
where the time goes in v3:
time: 142 us; the launch traced here: 141 us
  Pallas kernels  131 us (92%)
  local copies, waits for them, and re-layouts  7.95 us (6%)
    pallas_call x1, Pallas kernels, per_device(): pl.pallas_call(functools.partial(kernel if direct else halving_kernel, ex...  131 us
    unnamed x11, local copies, waits for them, and re-layouts  6.51 us

profile of v3, /device:TPU:12, one launch (start us, length us, event | category | flops | bytes accessed | tf_op | source)
XLA Modules:
  0.0 141.2 jit_solution(12709016118280849222)
XLA Ops:
  0.6 1.2 convert_bitcast_fusion.prob_t
  1.9 1.4 %copy.12.rout = s32[128,2]{1,0:T(8,128)} copy(s32[128,2]{0,1:T(2,128)} %param.8) | data formatting | bytes 2048 | tf_op args[1]
  3.3 131.4 %adasum_moe.1 = (f32[1,512,512]{2,1,0:T(8,128)}, f32[1,512,512]{2,1,0:T(8,128)}, f32[1,512,512]{2,1,0:T(8,128)}, bf16[128,2048]{1,0:T(8,128)(2,1)}, bf16[128,2]{1,0:T(8,128)(2,1)}) custom-call(bf16[128,2048]{1,0:T(8,128)(2,1)} %tok.1, bf16[128,2048]{1,0:T(8,128)(2,1)} %cot.1, s32[128,2]{1,0:T(8,128)} %copy.12.rout, s32[2,128]{1,0:T(2,128)} %bitcast.3, ...), custom_call_target="tpu_custom_call" | custom-call | tf_op jit(solution)/shard_map/adasum_moe/pallas_call | solution.py:780
  134.7 0.0 copy-start.1
  134.7 1.4 %copy.13 = bf16[128,2]{0,1:T(2,128)(2,1)} copy(bf16[128,2]{1,0:T(8,128)(2,1)} %get-tuple-element.9) | data formatting | bytes 1024 | tf_op jit(solution)/shard_map/adasum_moe/pallas_call | solution.py:780
  136.1 0.0 copy-start
  136.1 2.4 %copy.18 = f32[1,512,512]{2,1,0:T(8,128)} copy(f32[1,512,512]{2,1,0:T(8,128)} %get-tuple-element.15) | data formatting | bytes 2097152
  138.5 0.0 copy-done.1
  138.5 0.0 copy-start.2
  138.5 1.0 copy.19
  139.5 0.0 copy-done
  139.5 1.0 copy.20
  140.4 0.0 copy-done.2
  140.4 0.8 copy.21
Async XLA Ops:
  134.7 3.8 %copy-start.1 = (f32[1,512,512]{2,1,0:T(8,128)S(1)}, f32[1,512,512]{2,1,0:T(8,128)}, u32[]{:S(2)}) copy-start(f32[1,512,512]{2,1,0:T(8,128)} %get-tuple-element.16) | copy-start | bytes 3145732
  136.1 3.3 %copy-start = (f32[1,512,512]{2,1,0:T(8,128)S(1)}, f32[1,512,512]{2,1,0:T(8,128)}, u32[]{:S(2)}) copy-start(f32[1,512,512]{2,1,0:T(8,128)} %get-tuple-element.17) | copy-start | bytes 3145732
  138.5 1.9 %copy-start.2 = (bf16[128,2048]{1,0:T(8,128)(2,1)S(1)}, bf16[128,2048]{1,0:T(8,128)(2,1)}, u32[]{:S(2)}) copy-start(bf16[128,2048]{1,0:T(8,128)(2,1)} %get-tuple-element.18) | copy-start | bytes 1572868

commit v4 on v3

--- a/solution.py
+++ b/solution.py
@@ -733,11 +733,6 @@
         )
         copy.start()
         gram_copies.append(copy)
-    for copy in gram_copies:
-        copy.wait_recv()
-    for grad in (2, 1, 0):
-        combine(grad)
-
     for copy in ret_copies:
         copy.wait_recv()
 
@@ -753,6 +748,11 @@
         score = dot(select[rows, :], ret_recv[rows, width:], 0, 0)
         scores = scores + jnp.where(chosen_by == k, score[:, 0 : chosen_by.shape[1]], 0.0)
     out_router[...] = scores.astype(bf16)
+
+    for copy in gram_copies:
+        copy.wait_recv()
+    for grad in (2, 1, 0):
+        combine(grad)
 
     for copy in tok_copies + cot_copies + ret_copies + y_copies + gram_copies + core_copies:
         copy.wait_send()

time: 142 us -> 141 us (level)
  no operation moved by 1% of the time
where the time goes in v4:
time: 141 us; the launch traced here: 140 us
  Pallas kernels  130 us (92%)
  local copies, waits for them, and re-layouts  7.95 us (6%)
    pallas_call x1, Pallas kernels, per_device(): pl.pallas_call(functools.partial(kernel if direct else halving_kernel, ex...  130 us
    unnamed x11, local copies, waits for them, and re-layouts  6.51 us

profile of v4, /device:TPU:12, one launch (start us, length us, event | category | flops | bytes accessed | tf_op | source)
XLA Modules:
  0.0 140.0 jit_solution(4056224476420206995)
XLA Ops:
  0.6 1.2 convert_bitcast_fusion.prob_t
  1.9 1.4 %copy.12.rout = s32[128,2]{1,0:T(8,128)} copy(s32[128,2]{0,1:T(2,128)} %param.8) | data formatting | bytes 2048 | tf_op args[1]
  3.3 130.1 %adasum_moe.1 = (f32[1,512,512]{2,1,0:T(8,128)}, f32[1,512,512]{2,1,0:T(8,128)}, f32[1,512,512]{2,1,0:T(8,128)}, bf16[128,2048]{1,0:T(8,128)(2,1)}, bf16[128,2]{1,0:T(8,128)(2,1)}) custom-call(bf16[128,2048]{1,0:T(8,128)(2,1)} %tok.1, bf16[128,2048]{1,0:T(8,128)(2,1)} %cot.1, s32[128,2]{1,0:T(8,128)} %copy.12.rout, s32[2,128]{1,0:T(2,128)} %bitcast.3, ...), custom_call_target="tpu_custom_call" | custom-call | tf_op jit(solution)/shard_map/adasum_moe/pallas_call | solution.py:780
  133.4 0.0 copy-start.1
  133.4 1.4 %copy.13 = bf16[128,2]{0,1:T(2,128)(2,1)} copy(bf16[128,2]{1,0:T(8,128)(2,1)} %get-tuple-element.9) | data formatting | bytes 1024 | tf_op jit(solution)/shard_map/adasum_moe/pallas_call | solution.py:780
  134.9 0.0 copy-start
  134.9 2.4 %copy.18 = f32[1,512,512]{2,1,0:T(8,128)} copy(f32[1,512,512]{2,1,0:T(8,128)} %get-tuple-element.15) | data formatting | bytes 2097152
  137.2 0.0 copy-done.1
  137.2 0.0 copy-start.2
  137.2 1.0 copy.19
  138.2 0.0 copy-done
  138.2 1.0 copy.20
  139.2 0.0 copy-done.2
  139.2 0.8 copy.21
Async XLA Ops:
  133.4 3.8 %copy-start.1 = (f32[1,512,512]{2,1,0:T(8,128)S(1)}, f32[1,512,512]{2,1,0:T(8,128)}, u32[]{:S(2)}) copy-start(f32[1,512,512]{2,1,0:T(8,128)} %get-tuple-element.16) | copy-start | bytes 3145732
  134.9 3.3 %copy-start = (f32[1,512,512]{2,1,0:T(8,128)S(1)}, f32[1,512,512]{2,1,0:T(8,128)}, u32[]{:S(2)}) copy-start(f32[1,512,512]{2,1,0:T(8,128)} %get-tuple-element.17) | copy-start | bytes 3145732
  137.2 1.9 %copy-start.2 = (bf16[128,2048]{1,0:T(8,128)(2,1)S(1)}, bf16[128,2048]{1,0:T(8,128)(2,1)}, u32[]{:S(2)}) copy-start(bf16[128,2048]{1,0:T(8,128)(2,1)} %get-tuple-element.18) | copy-start | bytes 1572868
